TPU v7x, 128 devices: a whole 4x4x4 slice. The times are simulated.
128 devices in a mesh: rollout: 4 (over y_lo, core), row: 8 (over x, y_hi), col: 4 (over z).
Axes of the slice: x: 4, y: 4 (y_hi: 2, y_lo: 2; y = y_hi * 2 + y_lo), z: 4, core: 2. Of those that a mesh axis runs over, the one named last changes fastest.
Arguments:
- queries: bfloat16 [16384, 4096], P(('rollout', 'row', 'col')), may hold values from -16 to 16
- keys: bfloat16 [16384, 512], P(('rollout', 'row', 'col')), may hold values from -16 to 16
- values: bfloat16 [16384, 512], P(('rollout', 'row', 'col')), may hold values from -6 to 6
- out_grad: bfloat16 [16384, 4096], P(('rollout', 'row', 'col')), may hold values from -12 to 12
- hidden_in: bfloat16 [16384, 8192], P(('rollout', 'col'), 'row'), may hold values from -1.5 to 1.5
- q_weight: bfloat16 [4096, 8192], P('col', 'row'), may hold values from -0.09375 to 0.09375
- lengths: int32 [4, 32], P('rollout'), may hold values from 1 to 256, 4096 in all within a row
- kv_order: int32 [4], replicated, may hold values from 0 to 3, each once
Outputs:
- key_grad: float32 [16384, 512], P(('rollout', 'row', 'col'))
- value_grad: float32 [16384, 512], P(('rollout', 'row', 'col'))
- input_grad: bfloat16 [16384, 8192], P(('rollout', 'col'), 'row')
- weight_grad: float32 [4096, 8192], P(('rollout', 'col'), 'row')
Inputs may be any that keep to these rules, and one draw needn't show every extreme that they name: `lengths`: each row lists, for 16 packed rollouts in order, a prompt length and then a response length; a row sums to 4096 and its largest entry is exactly 256. `kv_order`: A permutation of the 4 key-value heads.
All inputs are finite; a program needn't handle non-finite values.
Results may differ from a plain program's by a relative error of at most 0.0057.
Values may be sent and summed in bfloat16 or wider, within the bound.
No kernel may reach another device: no remote copies, remote signals or barrier semaphores. Data moves between devices by JAX's collectives and lax.ppermute only.
A program may use at most 192 MiB of HBM per device.

v0:
```python
import math
import jax
import jax.numpy as jnp
from jax import lax
from jax.sharding import PartitionSpec as P

HQ = 32
KV = 4
HD = 128
ROLLS = 16


def token_parts(lengths_row, length_total):
    bounds = jnp.cumsum(lengths_row)
    position = jnp.arange(length_total, dtype=jnp.int32)
    return jnp.sum((position[:, None] >= bounds[None, :]).astype(jnp.int32), axis=1)


def attend_head(query_all, key_all, value_all, grad_all, document, row_block, reach):
    length_total = query_all.shape[0]
    scale_factor = 1.0 / math.sqrt(query_all.shape[1])
    position = jnp.arange(length_total, dtype=jnp.int32)
    grad_key = jnp.zeros(key_all.shape, jnp.float32)
    grad_value = jnp.zeros(value_all.shape, jnp.float32)
    query_pieces = []
    for row_begin in range(0, length_total, row_block):
        row_end = row_begin + row_block
        key_first = max(0, row_begin - reach)
        query_rows = query_all[row_begin:row_end]
        grad_rows = grad_all[row_begin:row_end]
        key_rows = key_all[key_first:row_end]
        value_rows = value_all[key_first:row_end]
        allowed = (position[None, key_first:row_end] <= position[row_begin:row_end, None]) & (
            document[None, key_first:row_end] == document[row_begin:row_end, None]
        )
        raw_scores = (
            jnp.einsum("qd,kd->qk", query_rows, key_rows, preferred_element_type=jnp.float32)
            * scale_factor
        )
        raw_scores = jnp.where(allowed, raw_scores, -jnp.inf)
        row_top = jnp.max(raw_scores, axis=1, keepdims=True)
        exp_scores = jnp.exp(raw_scores - row_top)
        attention = exp_scores / jnp.sum(exp_scores, axis=1, keepdims=True)
        attention_half = attention.astype(jnp.bfloat16)
        grad_value = grad_value.at[key_first:row_end].add(
            jnp.einsum("qk,qd->kd", attention_half, grad_rows, preferred_element_type=jnp.float32)
        )
        grad_attention = jnp.einsum(
            "qd,kd->qk", grad_rows, value_rows, preferred_element_type=jnp.float32
        )
        row_delta = jnp.sum(attention * grad_attention, axis=1, keepdims=True)
        grad_scores = (attention * (grad_attention - row_delta) * scale_factor).astype(jnp.bfloat16)
        query_pieces.append(
            jnp.dot(grad_scores, key_rows, preferred_element_type=jnp.float32).astype(jnp.bfloat16)
        )
        grad_key = grad_key.at[key_first:row_end].add(
            jnp.einsum("qk,qd->kd", grad_scores, query_rows, preferred_element_type=jnp.float32)
        )
    return (jnp.concatenate(query_pieces, axis=0), grad_key, grad_value)


def body(queries, keys, values, out_grad, hidden_in, q_weight, lengths, kv_order):
    group_size = lax.axis_size(("row", "col"))
    rows_count = lax.axis_size("row")
    columns_count = lax.axis_size("col")
    token_dev = queries.shape[0]
    length_total = token_dev * group_size
    heads_dev = HQ // group_size
    sources_each = HQ // KV // heads_dev
    reach = 2 * (length_total // ROLLS)
    head_query, head_grad = (
        lax.all_to_all(queries, ("row", "col"), split_axis=1, concat_axis=0, tiled=True),
        lax.all_to_all(out_grad, ("row", "col"), split_axis=1, concat_axis=0, tiled=True),
    )
    kv_range = jnp.arange(KV, dtype=jnp.int32)
    owner = jnp.arange(group_size, dtype=jnp.int32) // sources_each
    chosen = jnp.sum(jnp.where(owner[:, None] == kv_range[None, :], kv_order[None, :], 0), axis=1)
    pick_table = (kv_range[:, None] == chosen[None, :]).astype(jnp.bfloat16)
    key_send = jnp.einsum(
        "tkd,kj->tjd",
        keys.reshape(token_dev, KV, HD),
        pick_table,
        preferred_element_type=jnp.float32,
    ).astype(jnp.bfloat16)
    value_send = jnp.einsum(
        "tkd,kj->tjd",
        values.reshape(token_dev, KV, HD),
        pick_table,
        preferred_element_type=jnp.float32,
    ).astype(jnp.bfloat16)
    key_got, value_got = (
        lax.all_to_all(key_send, ("row", "col"), split_axis=1, concat_axis=0, tiled=True),
        lax.all_to_all(value_send, ("row", "col"), split_axis=1, concat_axis=0, tiled=True),
    )
    key_full = key_got.reshape(length_total, HD)
    value_full = value_got.reshape(length_total, HD)
    parts = token_parts(lengths[0], length_total)
    document = parts // 2
    response = (parts % 2).astype(jnp.bfloat16)
    head_grad = head_grad * response[:, None]
    row_block = min(512, length_total)
    grad_query, grad_key, grad_value = attend_head(
        head_query, key_full, value_full, head_grad, document, row_block, reach
    )
    key_back, value_back = (
        lax.all_to_all(
            grad_key.reshape(group_size, token_dev, HD),
            ("row", "col"),
            split_axis=0,
            concat_axis=0,
            tiled=True,
        ),
        lax.all_to_all(
            grad_value.reshape(group_size, token_dev, HD),
            ("row", "col"),
            split_axis=0,
            concat_axis=0,
            tiled=True,
        ),
    )
    order_table = (kv_order[:, None] == kv_range[None, :]).astype(jnp.float32)

    def place_heads(stacked):
        summed = jnp.sum(stacked.reshape(KV, sources_each, token_dev, HD), axis=1)
        placed = jnp.einsum("mtd,mk->tkd", summed, order_table, precision=lax.Precision.HIGHEST)
        return placed.reshape(token_dev, KV * HD)

    key_grad = place_heads(key_back)
    value_grad = place_heads(value_back)
    arranged = grad_query.reshape(columns_count, rows_count, token_dev, heads_dev * HD)
    arranged = arranged.transpose(1, 0, 2, 3).reshape(length_total, heads_dev * HD)
    shard_query = lax.all_to_all(arranged, ("row", "col"), split_axis=0, concat_axis=1, tiled=True)
    block_query = lax.all_gather(shard_query, "row", axis=0, tiled=True)
    used = block_query
    input_grad = jnp.dot(
        used,
        lax.all_gather(q_weight, "col", axis=0, tiled=True),
        preferred_element_type=jnp.float32,
    ).astype(jnp.bfloat16)
    used = block_query
    weight_grad = lax.psum_scatter(
        lax.dot_general(
            used, hidden_in, (((0,), (0,)), ((), ())), preferred_element_type=jnp.float32
        ),
        ("rollout", "col"),
        scatter_dimension=0,
        tiled=True,
    )
    return (key_grad, value_grad, input_grad, weight_grad)


def solution(mesh):
    placed = (
        P(("rollout", "row", "col"), None),
        P(("rollout", "row", "col"), None),
        P(("rollout", "row", "col"), None),
        P(("rollout", "row", "col"), None),
        P(("rollout", "col"), "row"),
        P("col", "row"),
        P("rollout", None),
        P(),
    )
    return jax.shard_map(
        body,
        mesh=mesh,
        in_specs=placed,
        out_specs=(
            P(("rollout", "row", "col"), None),
            P(("rollout", "row", "col"), None),
            P(("rollout", "col"), "row"),
            P(("rollout", "col"), "row"),
        ),
        check_vma=False,
    )
```

profile of v0, /device:TPU:1, one launch (start us, length us, event | category | flops | bytes accessed | tf_op | source)
XLA Modules:
  0.0 613.1 jit_solution(12362430108168158145)
XLA Ops:
  10.9 11.5 %all-to-all-start = ((bf16[128,32,128]{2,0,1:T(8,128)(2,1)}), bf16[128,32,128]{2,0,1:T(8,128)(2,1)S(1)}, u32[]{:S(2)}, u32[]{:S(2)}) async-start(bf16[128,32,128]{2,0,1:T(8,128)(2,1)} %copy.141), calls=%async_computation | async-start | bytes 2097152 | tf_op jit(solution)/shard_map/all_to_all | solution.py:92
  24.7 13.9 %all-to-all-done = bf16[128,32,128]{2,0,1:T(8,128)(2,1)S(1)} async-done(((bf16[128,32,128]{2,0,1:T(8,128)(2,1)}), bf16[128,32,128]{2,0,1:T(8,128)(2,1)S(1)}, u32[]{:S(2)}, u32[]{:S(2)}) %all-to-all-start) | async-done | bytes 1048608 | tf_op jit(solution)/shard_map/all_to_all | solution.py:92
  38.6 6.0 all-to-all-start.1
  46.4 2.6 copy.147
  56.5 3.5 all-to-all-done.1
  60.0 6.9 %all-to-all-start.3 = ((bf16[128,32,128]{2,0,1:T(8,128)(2,1)}), bf16[128,32,128]{2,0,1:T(8,128)(2,1)}, u32[]{:S(2)}, u32[]{:S(2)}) async-start(bf16[128,32,128]{2,0,1:T(8,128)(2,1)} %copy.147), calls=%async_computation.3 | async-start | bytes 2097152 | tf_op jit(solution)/shard_map/all_to_all | solution.py:93
  70.1 12.2 %all-to-all-done.3 = bf16[128,32,128]{2,0,1:T(8,128)(2,1)} async-done(((bf16[128,32,128]{2,0,1:T(8,128)(2,1)}), bf16[128,32,128]{2,0,1:T(8,128)(2,1)}, u32[]{:S(2)}, u32[]{:S(2)}) %all-to-all-start.3) | async-done | bytes 1048608 | tf_op jit(solution)/shard_map/all_to_all | solution.py:93
  82.3 6.9 %all-to-all-start.2 = ((bf16[128,32,128]{0,2,1:T(8,128)(2,1)}), bf16[128,32,128]{0,2,1:T(8,128)(2,1)}, u32[]{:S(2)}, u32[]{:S(2)}) async-start(bf16[128,32,128]{0,2,1:T(8,128)(2,1)} %bitcast.153), calls=%async_computation.2 | async-start | bytes 2097152 | tf_op jit(solution)/shard_map/all_to_all | solution.py:73
  95.7 2.8 fusion.102
  98.5 6.0 all-to-all-done.2
  146.6 22.1 %all_to_all.94 = bf16[32,128,128]{2,1,0:T(8,128)(2,1)} all-to-all(bf16[32,128,128]{2,1,0:T(8,128)(2,1)S(1)} %bitcast.156), channel_id=1, replica_groups=mesh['rollout'=4,'row'=8,'col'=4] {'row','col'}, dimensions={0} | all-to-all | bytes 2097152 | tf_op jit(solution)/shard_map/all_to_all | solution.py:132
  171.7 118.2 %all-gather.3.cloned.1.call-done = bf16[1024,4096]{0,1:T(8,128)(2,1)} async-done(((bf16[128,4096]{0,1:T(8,128)(2,1)}), bf16[1024,4096]{0,1:T(8,128)(2,1)}) %all-gather.3.cloned.1.call-update) | async-done | bytes 8388624 | tf_op jit(solution)/shard_map/all_gather | solution.py:133
  289.9 15.2 %fusion.114 = f32[4096,1024]{1,0:T(8,128)} fusion(bf16[1024,4096]{0,1:T(8,128)(2,1)} %all-gather.3.cloned.1.call-done, bf16[1024,1024]{1,0:T(8,128)(2,1)S(1)} %copy-done), kind=kOutput, calls=%fused_computation.197 | convolution fusion | flops 8589934592 | bytes 27262976 | tf_op jit(solution)/shard_map/dot_general | solution.py:142
  323.4 6.6 %all-to-all-start.4 = ((f32[32,128,128]{2,1,0:T(8,128)}), f32[32,128,128]{2,1,0:T(8,128)S(1)}, u32[]{:S(2)}, u32[]{:S(2)}) async-start(f32[32,128,128]{2,1,0:T(8,128)} %bitcast.48), calls=%async_computation.4 | async-start | bytes 4194304 | tf_op jit(solution)/shard_map/all_to_all | solution.py:106
  335.5 2.5 fusion.23
  338.0 2.5 fusion.22
  340.6 2.5 fusion.21
  343.1 2.5 fusion.20
  350.4 6.6 %all-to-all-done.4 = f32[32,128,128]{2,1,0:T(8,128)S(1)} async-done(((f32[32,128,128]{2,1,0:T(8,128)}), f32[32,128,128]{2,1,0:T(8,128)S(1)}, u32[]{:S(2)}, u32[]{:S(2)}) %all-to-all-start.4) | async-done | bytes 2097184 | tf_op jit(solution)/shard_map/all_to_all | solution.py:106
  357.0 10.1 %all-to-all-start.5 = ((f32[32,128,128]{2,1,0:T(8,128)}), f32[32,128,128]{2,1,0:T(8,128)}, u32[]{:S(2)}, u32[]{:S(2)}) async-start(f32[32,128,128]{2,1,0:T(8,128)} %bitcast.51), calls=%async_computation.5 | async-start | bytes 4194304 | tf_op jit(solution)/shard_map/all_to_all | solution.py:113
  369.0 26.8 %all-to-all-done.5 = f32[32,128,128]{2,1,0:T(8,128)} async-done(((f32[32,128,128]{2,1,0:T(8,128)}), f32[32,128,128]{2,1,0:T(8,128)}, u32[]{:S(2)}, u32[]{:S(2)}) %all-to-all-start.5) | async-done | bytes 2097184 | tf_op jit(solution)/shard_map/all_to_all | solution.py:113
  398.8 21.5 %all-gather.5.cloned.1.call-done = bf16[4096,1024]{1,0:T(8,128)(2,1)} async-done(((bf16[1024,1024]{1,0:T(8,128)(2,1)}), bf16[4096,1024]{1,0:T(8,128)(2,1)}) %all-gather.5.cloned.1.call-update) | async-done | bytes 8388624 | tf_op jit(solution)/shard_map/all_gather | solution.py:137
  420.3 14.8 %convolution_convert_fusion = bf16[1024,1024]{1,0:T(8,128)(2,1)} fusion(bf16[1024,4096]{0,1:T(8,128)(2,1)} %all-gather.3.cloned.1.call-done, bf16[4096,1024]{1,0:T(8,128)(2,1)} %all-gather.5.cloned.1.call-done), kind=kOutput, calls=%fused_computation.30 | convolution fusion | flops 8590983168 | bytes 18874368 | tf_op jit(solution)/shard_map/dot_general | solution.py:135
  435.1 171.2 %reduce-scatter.2.cloned.1.call-done = f32[256,1024]{1,0:T(8,128)} async-done(((f32[4096,1024]{1,0:T(8,128)}), f32[256,1024]{1,0:T(8,128)}) %reduce-scatter.2.cloned.1.call-update) | async-done | bytes 1048592 | tf_op jit(solution)/shard_map/reduce_scatter | solution.py:141
  (347 shorter events, 102.5 us)
Async XLA Ops:
  7.2 282.7 %copy-start = (bf16[1024,1024]{1,0:T(8,128)(2,1)S(1)}, bf16[1024,1024]{1,0:T(8,128)(2,1)}, u32[]{:S(2)}) copy-start(bf16[1024,1024]{1,0:T(8,128)(2,1)} %param.44) | copy-start | bytes 6291460
  10.9 13.8 %copy-start.62 = (bf16[128,512]{1,0:T(8,128)(2,1)S(1)}, bf16[128,512]{1,0:T(8,128)(2,1)}, u32[]{:S(2)}) copy-start(bf16[128,512]{1,0:T(8,128)(2,1)} %param.42) | copy-start | bytes 393220
  10.9 27.7 %all-to-all-start = ((bf16[128,32,128]{2,0,1:T(8,128)(2,1)}), bf16[128,32,128]{2,0,1:T(8,128)(2,1)S(1)}, u32[]{:S(2)}, u32[]{:S(2)}) async-start(bf16[128,32,128]{2,0,1:T(8,128)(2,1)} %copy.141), calls=%async_computation | async-start | bytes 2097152 | tf_op jit(solution)/shard_map/all_to_all | solution.py:92
  24.7 21.5 %copy-start.117 = (s32[1,32]{1,0:T(1,128)S(1)}, s32[1,32]{1,0:T(1,128)}, u32[]{:S(2)}) copy-start(s32[1,32]{1,0:T(1,128)} %param.46) | copy-start | bytes 388
  38.6 21.4 %all-to-all-start.1 = ((bf16[128,32,128]{0,2,1:T(8,128)(2,1)}), bf16[128,32,128]{0,2,1:T(8,128)(2,1)}, u32[]{:S(2)}, u32[]{:S(2)}) async-start(bf16[128,32,128]{0,2,1:T(8,128)(2,1)} %bitcast.154), calls=%async_computation.1 | async-start | bytes 2097152 | tf_op jit(solution)/shard_map/all_to_all | solution.py:72
  60.0 22.2 %all-to-all-start.3 = ((bf16[128,32,128]{2,0,1:T(8,128)(2,1)}), bf16[128,32,128]{2,0,1:T(8,128)(2,1)}, u32[]{:S(2)}, u32[]{:S(2)}) async-start(bf16[128,32,128]{2,0,1:T(8,128)(2,1)} %copy.147), calls=%async_computation.3 | async-start | bytes 2097152 | tf_op jit(solution)/shard_map/all_to_all | solution.py:93
  82.3 22.2 %all-to-all-start.2 = ((bf16[128,32,128]{0,2,1:T(8,128)(2,1)}), bf16[128,32,128]{0,2,1:T(8,128)(2,1)}, u32[]{:S(2)}, u32[]{:S(2)}) async-start(bf16[128,32,128]{0,2,1:T(8,128)(2,1)} %bitcast.153), calls=%async_computation.2 | async-start | bytes 2097152 | tf_op jit(solution)/shard_map/all_to_all | solution.py:73
  89.1 200.8 %all-gather.3.cloned.1.call-start = ((), (), s32[]{:S(2)}) async-start(), calls=%async_computation.8 | async-start | bytes 9437184 | tf_op jit(solution)/shard_map/all_gather | solution.py:133
  120.6 20.5 %copy-start.38 = (bf16[4096,128]{1,0:T(8,128)(2,1)}, bf16[4096,128]{1,0:T(8,128)(2,1)S(1)}, u32[]{:S(2)}) copy-start(bf16[4096,128]{1,0:T(8,128)(2,1)S(1)} %bitcast_multiply_fusion) | copy-start | bytes 3145732
  127.9 15.3 %copy-start.2 = (bf16[512,1024]{0,1:T(8,128)(2,1)}, bf16[512,1024]{0,1:T(8,128)(2,1)S(1)}, u32[]{:S(2)}) copy-start(bf16[512,1024]{0,1:T(8,128)(2,1)S(1)} %multiply_convert_fusion.5) | copy-start | bytes 3145732
  130.8 13.0 %copy-start.4 = (bf16[512,1024]{0,1:T(8,128)(2,1)}, bf16[512,1024]{0,1:T(8,128)(2,1)S(1)}, u32[]{:S(2)}) copy-start(bf16[512,1024]{0,1:T(8,128)(2,1)S(1)} %multiply_convert_fusion.4) | copy-start | bytes 3145732
  133.8 10.5 %copy-start.6 = (bf16[512,1024]{0,1:T(8,128)(2,1)}, bf16[512,1024]{0,1:T(8,128)(2,1)S(1)}, u32[]{:S(2)}) copy-start(bf16[512,1024]{0,1:T(8,128)(2,1)S(1)} %multiply_convert_fusion.3) | copy-start | bytes 3145732
  136.7 8.1 %copy-start.8 = (bf16[512,1024]{0,1:T(8,128)(2,1)}, bf16[512,1024]{0,1:T(8,128)(2,1)S(1)}, u32[]{:S(2)}) copy-start(bf16[512,1024]{0,1:T(8,128)(2,1)S(1)} %multiply_convert_fusion.2) | copy-start | bytes 3145732
  139.9 5.6 copy-start.10
  170.9 249.3 %all-gather.5.cloned.1.call-start = ((), (), s32[]{:S(2)}) async-start(), calls=%async_computation.9 | async-start | bytes 10485760 | tf_op jit(solution)/shard_map/all_gather | solution.py:137
  171.7 434.6 %reduce-scatter.2.cloned.1.call-start = ((), (), s32[]{:S(2)}) async-start(), calls=%async_computation.10 | async-start | bytes 17825792 | tf_op jit(solution)/shard_map/reduce_scatter | solution.py:141
  311.6 4.8 copy-start.9
  311.6 4.8 copy-start.45
  314.0 4.8 copy-start.11
  314.0 4.8 copy-start.43
  323.3 6.6 %copy-start.31 = (f32[512,512]{0,1:T(8,128)S(1)}, f32[512,512]{0,1:T(8,128)}, u32[]{:S(2)}) copy-start(f32[512,512]{0,1:T(8,128)} %copy-done.30) | copy-start | bytes 3145732
  323.4 33.7 %all-to-all-start.4 = ((f32[32,128,128]{2,1,0:T(8,128)}), f32[32,128,128]{2,1,0:T(8,128)S(1)}, u32[]{:S(2)}, u32[]{:S(2)}) async-start(f32[32,128,128]{2,1,0:T(8,128)} %bitcast.48), calls=%async_computation.4 | async-start | bytes 4194304 | tf_op jit(solution)/shard_map/all_to_all | solution.py:106
  357.0 38.8 %all-to-all-start.5 = ((f32[32,128,128]{2,1,0:T(8,128)}), f32[32,128,128]{2,1,0:T(8,128)}, u32[]{:S(2)}, u32[]{:S(2)}) async-start(f32[32,128,128]{2,1,0:T(8,128)} %bitcast.51), calls=%async_computation.5 | async-start | bytes 4194304 | tf_op jit(solution)/shard_map/all_to_all | solution.py:113
  420.3 186.0 %copy-start.1 = (bf16[1024,1024]{1,0:T(8,128)(2,1)S(1)}, bf16[1024,1024]{1,0:T(8,128)(2,1)}, u32[]{:S(2)}) copy-start(bf16[1024,1024]{1,0:T(8,128)(2,1)} %param.44) | copy-start | bytes 6291460
  (103 other events, 164.8 us)
Sparse Core Ops, SparseCore 0:
  171.1 118.8 all-gather.2
  291.6 128.6 all-gather.4
  423.2 182.9 reduce-scatter.1
where the time goes:
time: 620 us; the launch traced here: 613 us
  waiting for transfers between devices  381 us (61%)
  matrix products  79.8 us (13%)
  starting transfers between devices  48 us (8%)
  local copies, waits for them, and re-layouts  47.1 us (8%)
  blocking collectives  22.1 us (4%)
  other arithmetic  20.2 us (3%)
  between operations  15.2 us (2%)
    reduce_scatter x1, waiting for transfers between devices, body(): lax.psum_scatter(lax.dot_general(used, hidden_in, (((0,), (0,)), ((), ())...  171 us
    all_gather x1, waiting for transfers between devices, body(): block_query = lax.all_gather(shard_query, 'row', axis=0, tiled=True)  118 us
    all_to_all x1, waiting for transfers between devices, body(): lax.all_to_all(grad_value.reshape(group_size, token_dev, HD), ('row', 'co...  26.8 us
    all_to_all x1, blocking collectives, body(): lax.all_to_all(arranged, ('row', 'col'), split_axis=0, concat_axis=1, til...  22.1 us
    all_gather x1, waiting for transfers between devices, body(): lax.all_gather(q_weight, 'col', axis=0, tiled=True)  21.5 us
    dot_general x8, matrix products, attend_head(): jnp.einsum('qk,qd->kd', attention_half, grad_rows, preferred_element_type...  17.4 us
    dot_general x8, matrix products, attend_head(): jnp.einsum('qk,qd->kd', grad_scores, query_rows, preferred_element_type=j...  15.5 us
    dot_general x1, matrix products, body(): lax.dot_general(used, hidden_in, (((0,), (0,)), ((), ())), preferred_elem...  15.2 us
  transfers between devices with their start and end apart: 9, of which 9 were waited for; matrix products, arithmetic and copies ran while one was open for 16% of the time, Pallas kernels for 0%

commit v1 on v0

--- a/solution.py
+++ b/solution.py
@@ -1,3 +1,4 @@
+import functools
 import math
 import jax
 import jax.numpy as jnp
@@ -8,6 +9,16 @@
 KV = 4
 HD = 128
 ROLLS = 16
+
+
+def replace_screen(mine_x, device_axis, dim_no):
+    top = jnp.stack([mine_x for _ in range(lax.psum(1, device_axis))], axis=0)
+    ready = lax.all_to_all(top, device_axis, 0, 0)
+    y = jnp.concatenate(ready, axis=dim_no)
+    return y
+
+
+kinds_prepare = functools.partial(replace_screen, device_axis="row", dim_no=0)
 
 
 def token_parts(lengths_row, length_total):
@@ -130,7 +141,7 @@
     arranged = grad_query.reshape(columns_count, rows_count, token_dev, heads_dev * HD)
     arranged = arranged.transpose(1, 0, 2, 3).reshape(length_total, heads_dev * HD)
     shard_query = lax.all_to_all(arranged, ("row", "col"), split_axis=0, concat_axis=1, tiled=True)
-    block_query = lax.all_gather(shard_query, "row", axis=0, tiled=True)
+    block_query = kinds_prepare(shard_query)
     used = block_query
     input_grad = jnp.dot(
         used,

time: 620 us -> 531 us (0.86)
  waiting for transfers between devices: 381 us -> 192 us
  blocking collectives: 22.1 us -> 121 us
    all_gather x1 -> x0, waiting for transfers between devices: 118 us -> none  [body(): block_query = lax.all_gather(shard_query, 'row', axis=0, tiled=True)]
    all_to_all x0 -> x1, blocking collectives: none -> 97.4 us  [replace_screen(): ready = lax.all_to_all(top, device_axis, 0, 0)]
    reduce_scatter x1, waiting for transfers between devices: 171 us -> 118 us  [body(): lax.psum_scatter(lax.dot_general(used, hidden_in, (((0,), (0,)), ((), ())...]
    all_gather x1, waiting for transfers between devices: 21.5 us -> 0.01 us  [body(): lax.all_gather(q_weight, 'col', axis=0, tiled=True)]
    slice x9, local copies, waits for them, and re-layouts: 14 us -> 7.76 us  [attend_head(): query_rows = query_all[row_begin:row_end]]
    unnamed x240 -> x254, local copies, waits for them, and re-layouts: 14.8 us -> 13.2 us
  transfers between devices with their start and end apart: 9 -> 8, of which waited for: 9 -> 7; matrix products, arithmetic and copies ran while one was open for 16% -> 25% of each run, Pallas kernels for 0% -> 0%
where the time goes in v1:
time: 531 us; the launch traced here: 524 us
  waiting for transfers between devices  192 us (36%)
  blocking collectives  121 us (23%)
  matrix products  78.2 us (15%)
  starting transfers between devices  49.4 us (9%)
  local copies, waits for them, and re-layouts  44.4 us (8%)
  other arithmetic  21.5 us (4%)
  between operations  17.1 us (3%)
    reduce_scatter x1, waiting for transfers between devices, body(): lax.psum_scatter(lax.dot_general(used, hidden_in, (((0,), (0,)), ((), ())...  118 us
    all_to_all x1, blocking collectives, replace_screen(): ready = lax.all_to_all(top, device_axis, 0, 0)  97.4 us
    all_to_all x1, waiting for transfers between devices, body(): lax.all_to_all(grad_value.reshape(group_size, token_dev, HD), ('row', 'co...  28 us
    all_to_all x1, blocking collectives, body(): lax.all_to_all(arranged, ('row', 'col'), split_axis=0, concat_axis=1, til...  24 us
    dot_general x8, matrix products, attend_head(): jnp.einsum('qk,qd->kd', attention_half, grad_rows, preferred_element_type...  16.4 us
    dot_general x8, matrix products, attend_head(): jnp.einsum('qk,qd->kd', grad_scores, query_rows, preferred_element_type=j...  15.6 us
    dot_general x1, matrix products, body(): jnp.dot(used, lax.all_gather(q_weight, 'col', axis=0, tiled=True), prefer...  14.8 us
    dot_general x1, matrix products, body(): lax.dot_general(used, hidden_in, (((0,), (0,)), ((), ())), preferred_elem...  14.6 us
  transfers between devices with their start and end apart: 8, of which 7 were waited for; matrix products, arithmetic and copies ran while one was open for 25% of the time, Pallas kernels for 0%

profile of v1, /device:TPU:1, one launch (start us, length us, event | category | flops | bytes accessed | tf_op | source)
XLA Modules:
  0.0 524.3 jit_solution(7791121332718608042)
XLA Ops:
  11.7 11.3 %all-to-all-start = ((bf16[128,32,128]{2,0,1:T(8,128)(2,1)}), bf16[128,32,128]{2,0,1:T(8,128)(2,1)S(1)}, u32[]{:S(2)}, u32[]{:S(2)}) async-start(bf16[128,32,128]{2,0,1:T(8,128)(2,1)} %copy.144), calls=%async_computation | async-start | bytes 2097152 | tf_op jit(solution)/shard_map/all_to_all | solution.py:103
  26.2 13.2 %all-to-all-done = bf16[128,32,128]{2,0,1:T(8,128)(2,1)S(1)} async-done(((bf16[128,32,128]{2,0,1:T(8,128)(2,1)}), bf16[128,32,128]{2,0,1:T(8,128)(2,1)S(1)}, u32[]{:S(2)}, u32[]{:S(2)}) %all-to-all-start) | async-done | bytes 1048608 | tf_op jit(solution)/shard_map/all_to_all | solution.py:103
  39.3 6.0 %all-to-all-start.1 = ((bf16[128,32,128]{0,2,1:T(8,128)(2,1)}), bf16[128,32,128]{0,2,1:T(8,128)(2,1)}, u32[]{:S(2)}, u32[]{:S(2)}) async-start(bf16[128,32,128]{0,2,1:T(8,128)(2,1)} %bitcast.157), calls=%async_computation.1 | async-start | bytes 2097152 | tf_op jit(solution)/shard_map/all_to_all | solution.py:83
  47.1 2.6 copy.150
  57.3 3.5 all-to-all-done.1
  60.7 8.6 %all-to-all-start.3 = ((bf16[128,32,128]{2,0,1:T(8,128)(2,1)}), bf16[128,32,128]{2,0,1:T(8,128)(2,1)}, u32[]{:S(2)}, u32[]{:S(2)}) async-start(bf16[128,32,128]{2,0,1:T(8,128)(2,1)} %copy.150), calls=%async_computation.3 | async-start | bytes 2097152 | tf_op jit(solution)/shard_map/all_to_all | solution.py:104
  72.6 12.9 %all-to-all-done.3 = bf16[128,32,128]{2,0,1:T(8,128)(2,1)} async-done(((bf16[128,32,128]{2,0,1:T(8,128)(2,1)}), bf16[128,32,128]{2,0,1:T(8,128)(2,1)}, u32[]{:S(2)}, u32[]{:S(2)}) %all-to-all-start.3) | async-done | bytes 1048608 | tf_op jit(solution)/shard_map/all_to_all | solution.py:104
  85.5 8.1 %all-to-all-start.2 = ((bf16[128,32,128]{0,2,1:T(8,128)(2,1)}), bf16[128,32,128]{0,2,1:T(8,128)(2,1)}, u32[]{:S(2)}, u32[]{:S(2)}) async-start(bf16[128,32,128]{0,2,1:T(8,128)(2,1)} %bitcast.156), calls=%async_computation.2 | async-start | bytes 2097152 | tf_op jit(solution)/shard_map/all_to_all | solution.py:84
  100.1 2.8 fusion.102
  102.9 7.0 %all-to-all-done.2 = bf16[128,32,128]{0,2,1:T(8,128)(2,1)} async-done(((bf16[128,32,128]{0,2,1:T(8,128)(2,1)}), bf16[128,32,128]{0,2,1:T(8,128)(2,1)}, u32[]{:S(2)}, u32[]{:S(2)}) %all-to-all-start.2) | async-done | bytes 1048608 | tf_op jit(solution)/shard_map/all_to_all | solution.py:84
  146.5 24.0 %all_to_all.96 = bf16[32,128,128]{2,1,0:T(8,128)(2,1)} all-to-all(bf16[32,128,128]{2,1,0:T(8,128)(2,1)S(1)} %bitcast.158), channel_id=1, replica_groups=mesh['rollout'=4,'row'=8,'col'=4] {'row','col'}, dimensions={0} | all-to-all | bytes 2097152 | tf_op jit(solution)/shard_map/all_to_all | solution.py:143
  177.3 97.4 %all_to_all.97 = bf16[8,128,4096]{2,1,0:T(8,128)(2,1)} all-to-all(bf16[8,128,4096]{2,1,0:T(8,128)(2,1)S(1)} %stack.5), channel_id=1, replica_groups=mesh['rollout'=4,'row'=8,'col'=4] {'row'}, dimensions={0} | all-to-all | bytes 16777216 | tf_op jit(solution)/shard_map/all_to_all | solution.py:16
  274.8 14.6 %fusion.114 = f32[4096,1024]{1,0:T(8,128)} fusion(bf16[1024,4096]{1,0:T(8,128)(2,1)} %bitcast.154, bf16[1024,1024]{1,0:T(8,128)(2,1)S(1)} %copy-done), kind=kOutput, calls=%fused_computation.197 | convolution fusion | flops 8589934592 | bytes 27262976 | tf_op jit(solution)/shard_map/dot_general | solution.py:153
  307.6 5.6 %all-to-all-start.4 = ((f32[32,128,128]{2,1,0:T(8,128)}), f32[32,128,128]{2,1,0:T(8,128)}, u32[]{:S(2)}, u32[]{:S(2)}) async-start(f32[32,128,128]{2,1,0:T(8,128)} %bitcast.48), calls=%async_computation.4 | async-start | bytes 4194304 | tf_op jit(solution)/shard_map/all_to_all | solution.py:117
  317.7 2.5 fusion.23
  320.2 2.5 fusion.22
  322.8 2.5 fusion.21
  325.3 2.5 fusion.20
  327.9 2.5 fusion.19
  332.7 8.9 %all-to-all-done.4 = f32[32,128,128]{2,1,0:T(8,128)} async-done(((f32[32,128,128]{2,1,0:T(8,128)}), f32[32,128,128]{2,1,0:T(8,128)}, u32[]{:S(2)}, u32[]{:S(2)}) %all-to-all-start.4) | async-done | bytes 2097184 | tf_op jit(solution)/shard_map/all_to_all | solution.py:117
  341.5 9.7 %all-to-all-start.5 = ((f32[32,128,128]{2,1,0:T(8,128)}), f32[32,128,128]{2,1,0:T(8,128)S(1)}, u32[]{:S(2)}, u32[]{:S(2)}) async-start(f32[32,128,128]{2,1,0:T(8,128)} %bitcast.51), calls=%async_computation.5 | async-start | bytes 4194304 | tf_op jit(solution)/shard_map/all_to_all | solution.py:124
  354.2 28.0 %all-to-all-done.5 = f32[32,128,128]{2,1,0:T(8,128)S(1)} async-done(((f32[32,128,128]{2,1,0:T(8,128)}), f32[32,128,128]{2,1,0:T(8,128)S(1)}, u32[]{:S(2)}, u32[]{:S(2)}) %all-to-all-start.5) | async-done | bytes 2097184 | tf_op jit(solution)/shard_map/all_to_all | solution.py:124
  383.5 14.8 %convolution_convert_fusion = bf16[1024,1024]{1,0:T(8,128)(2,1)} fusion(bf16[1024,4096]{1,0:T(8,128)(2,1)} %bitcast.155, bf16[4096,1024]{1,0:T(8,128)(2,1)} %all-gather.2.cloned.1.call-done), kind=kOutput, calls=%fused_computation.30 | convolution fusion | flops 8590983168 | bytes 18874368 | tf_op jit(solution)/shard_map/dot_general | solution.py:146
  398.3 118.3 %reduce-scatter.2.cloned.1.call-done = f32[256,1024]{1,0:T(8,128)} async-done(((f32[4096,1024]{1,0:T(8,128)}), f32[256,1024]{1,0:T(8,128)}) %reduce-scatter.2.cloned.1.call-update) | async-done | bytes 1048592 | tf_op jit(solution)/shard_map/reduce_scatter | solution.py:152
  (361 shorter events, 97.6 us)
Async XLA Ops:
  8.0 266.8 %copy-start = (bf16[1024,1024]{1,0:T(8,128)(2,1)S(1)}, bf16[1024,1024]{1,0:T(8,128)(2,1)}, u32[]{:S(2)}) copy-start(bf16[1024,1024]{1,0:T(8,128)(2,1)} %param.44) | copy-start | bytes 6291460
  11.7 27.6 %all-to-all-start = ((bf16[128,32,128]{2,0,1:T(8,128)(2,1)}), bf16[128,32,128]{2,0,1:T(8,128)(2,1)S(1)}, u32[]{:S(2)}, u32[]{:S(2)}) async-start(bf16[128,32,128]{2,0,1:T(8,128)(2,1)} %copy.144), calls=%async_computation | async-start | bytes 2097152 | tf_op jit(solution)/shard_map/all_to_all | solution.py:103
  23.1 360.4 %all-gather.2.cloned.1.call-start = ((), (), s32[]{:S(2)}) async-start(), calls=%async_computation.9 | async-start | bytes 10485760 | tf_op jit(solution)/shard_map/all_gather | solution.py:148
  26.1 20.7 %copy-start.124 = (s32[1,32]{1,0:T(1,128)S(1)}, s32[1,32]{1,0:T(1,128)}, u32[]{:S(2)}) copy-start(s32[1,32]{1,0:T(1,128)} %param.46) | copy-start | bytes 388
  39.3 21.4 %all-to-all-start.1 = ((bf16[128,32,128]{0,2,1:T(8,128)(2,1)}), bf16[128,32,128]{0,2,1:T(8,128)(2,1)}, u32[]{:S(2)}, u32[]{:S(2)}) async-start(bf16[128,32,128]{0,2,1:T(8,128)(2,1)} %bitcast.157), calls=%async_computation.1 | async-start | bytes 2097152 | tf_op jit(solution)/shard_map/all_to_all | solution.py:83
  60.7 24.7 %all-to-all-start.3 = ((bf16[128,32,128]{2,0,1:T(8,128)(2,1)}), bf16[128,32,128]{2,0,1:T(8,128)(2,1)}, u32[]{:S(2)}, u32[]{:S(2)}) async-start(bf16[128,32,128]{2,0,1:T(8,128)(2,1)} %copy.150), calls=%async_computation.3 | async-start | bytes 2097152 | tf_op jit(solution)/shard_map/all_to_all | solution.py:104
  85.5 24.4 %all-to-all-start.2 = ((bf16[128,32,128]{0,2,1:T(8,128)(2,1)}), bf16[128,32,128]{0,2,1:T(8,128)(2,1)}, u32[]{:S(2)}, u32[]{:S(2)}) async-start(bf16[128,32,128]{0,2,1:T(8,128)(2,1)} %bitcast.156), calls=%async_computation.2 | async-start | bytes 2097152 | tf_op jit(solution)/shard_map/all_to_all | solution.py:84
  93.5 423.1 %reduce-scatter.2.cloned.1.call-start = ((), (), s32[]{:S(2)}) async-start(), calls=%async_computation.10 | async-start | bytes 17825792 | tf_op jit(solution)/shard_map/reduce_scatter | solution.py:152
  100.1 12.1 %copy-start.58 = (bf16[4,128,128]{1,2,0:T(8,128)(2,1)S(1)}, bf16[4,128,128]{1,2,0:T(8,128)(2,1)}, u32[]{:S(2)}) copy-start(bf16[4,128,128]{1,2,0:T(8,128)(2,1)} %get-tuple-element.202) | copy-start | bytes 393220
  102.9 10.0 %copy-start.57 = (bf16[4,128,128]{1,2,0:T(8,128)(2,1)S(1)}, bf16[4,128,128]{1,2,0:T(8,128)(2,1)}, u32[]{:S(2)}) copy-start(bf16[4,128,128]{1,2,0:T(8,128)(2,1)} %get-tuple-element.201) | copy-start | bytes 393220
  102.9 10.8 %copy-start.56 = (bf16[4,128,128]{1,2,0:T(8,128)(2,1)S(1)}, bf16[4,128,128]{1,2,0:T(8,128)(2,1)}, u32[]{:S(2)}) copy-start(bf16[4,128,128]{1,2,0:T(8,128)(2,1)} %get-tuple-element.200) | copy-start | bytes 393220
  102.9 11.6 %copy-start.55 = (bf16[4,128,128]{1,2,0:T(8,128)(2,1)S(1)}, bf16[4,128,128]{1,2,0:T(8,128)(2,1)}, u32[]{:S(2)}) copy-start(bf16[4,128,128]{1,2,0:T(8,128)(2,1)} %get-tuple-element.199) | copy-start | bytes 393220
  102.9 12.3 %copy-start.54 = (bf16[4,128,128]{1,2,0:T(8,128)(2,1)S(1)}, bf16[4,128,128]{1,2,0:T(8,128)(2,1)}, u32[]{:S(2)}) copy-start(bf16[4,128,128]{1,2,0:T(8,128)(2,1)} %get-tuple-element.198) | copy-start | bytes 393220
  102.9 13.1 %copy-start.53 = (bf16[4,128,128]{1,2,0:T(8,128)(2,1)S(1)}, bf16[4,128,128]{1,2,0:T(8,128)(2,1)}, u32[]{:S(2)}) copy-start(bf16[4,128,128]{1,2,0:T(8,128)(2,1)} %get-tuple-element.197) | copy-start | bytes 393220
  102.9 13.9 %copy-start.52 = (bf16[4,128,128]{1,2,0:T(8,128)(2,1)S(1)}, bf16[4,128,128]{1,2,0:T(8,128)(2,1)}, u32[]{:S(2)}) copy-start(bf16[4,128,128]{1,2,0:T(8,128)(2,1)} %get-tuple-element.196) | copy-start | bytes 393220
  121.5 23.2 %copy-start.38 = (bf16[4096,128]{1,0:T(8,128)(2,1)}, bf16[4096,128]{1,0:T(8,128)(2,1)S(1)}, u32[]{:S(2)}) copy-start(bf16[4096,128]{1,0:T(8,128)(2,1)S(1)} %bitcast_multiply_fusion) | copy-start | bytes 3145732
  128.8 12.0 %copy-start.2 = (bf16[512,1024]{0,1:T(8,128)(2,1)}, bf16[512,1024]{0,1:T(8,128)(2,1)S(1)}, u32[]{:S(2)}) copy-start(bf16[512,1024]{0,1:T(8,128)(2,1)S(1)} %multiply_convert_fusion.5) | copy-start | bytes 3145732
  131.7 9.6 %copy-start.4 = (bf16[512,1024]{0,1:T(8,128)(2,1)}, bf16[512,1024]{0,1:T(8,128)(2,1)S(1)}, u32[]{:S(2)}) copy-start(bf16[512,1024]{0,1:T(8,128)(2,1)S(1)} %multiply_convert_fusion.4) | copy-start | bytes 3145732
  134.7 7.2 %copy-start.6 = (bf16[512,1024]{0,1:T(8,128)(2,1)}, bf16[512,1024]{0,1:T(8,128)(2,1)S(1)}, u32[]{:S(2)}) copy-start(bf16[512,1024]{0,1:T(8,128)(2,1)S(1)} %multiply_convert_fusion.3) | copy-start | bytes 3145732
  145.9 24.6 %copy-start.12 = (bf16[512,1024]{0,1:T(8,128)(2,1)}, bf16[512,1024]{0,1:T(8,128)(2,1)S(1)}, u32[]{:S(2)}) copy-start(bf16[512,1024]{0,1:T(8,128)(2,1)S(1)} %multiply_convert_fusion) | copy-start | bytes 3145732
  307.6 5.6 %copy-start.39 = (bf16[4096,128]{1,0:T(8,128)(2,1)S(1)}, bf16[4096,128]{1,0:T(8,128)(2,1)}, u32[]{:S(2)}) copy-start(bf16[4096,128]{1,0:T(8,128)(2,1)} %copy-done.38) | copy-start | bytes 3145732
  307.6 34.0 %all-to-all-start.4 = ((f32[32,128,128]{2,1,0:T(8,128)}), f32[32,128,128]{2,1,0:T(8,128)}, u32[]{:S(2)}, u32[]{:S(2)}) async-start(f32[32,128,128]{2,1,0:T(8,128)} %bitcast.48), calls=%async_computation.4 | async-start | bytes 4194304 | tf_op jit(solution)/shard_map/all_to_all | solution.py:117
  341.5 40.6 %all-to-all-start.5 = ((f32[32,128,128]{2,1,0:T(8,128)}), f32[32,128,128]{2,1,0:T(8,128)S(1)}, u32[]{:S(2)}, u32[]{:S(2)}) async-start(f32[32,128,128]{2,1,0:T(8,128)} %bitcast.51), calls=%async_computation.5 | async-start | bytes 4194304 | tf_op jit(solution)/shard_map/all_to_all | solution.py:124
  383.5 133.1 %copy-start.1 = (bf16[1024,1024]{1,0:T(8,128)(2,1)S(1)}, bf16[1024,1024]{1,0:T(8,128)(2,1)}, u32[]{:S(2)}) copy-start(bf16[1024,1024]{1,0:T(8,128)(2,1)} %param.44) | copy-start | bytes 6291460
  (109 other events, 220.3 us)
Sparse Core Ops, SparseCore 0:
  25.6 118.6 all-gather.1
Sparse Core Ops, SparseCore 1:
  289.5 227.0 reduce-scatter.1
